TPU v7x, 256 devices: a whole 4x4x8 slice. The times are simulated.
256 devices in a mesh: slab: 64 (over z, y, core), col: 4 (over x).
Axes of the slice: x: 4, y: 4, z: 8, core: 2. Of those that a mesh axis runs over, the one named last changes fastest.
Arguments:
- recycle_basis: float32 [16, 3, 128, 8, 256], P('col', None, 'slab'), may hold values from -400 to 400
- densities: float32 [128, 8, 256], P('slab'), may hold values from 0.2 to 1
- solid_mask: int32 [128, 8, 256], P('slab'), may hold values 0 or 1
- fixed_mask: int32 [128, 8, 256], P('slab'), may hold values 0 or 1
Outputs:
- ortho_basis: float32 [16, 3, 128, 8, 256], P('col', None, 'slab')
- new_recycle: float32 [16, 3, 128, 8, 256], P('col', None, 'slab')
- r_factor: float32 [16, 16], replicated
Inputs may be any that keep to these rules, and one draw needn't show every extreme that they name: `solid_mask`: 1 marks a solid lattice voxel. `fixed_mask`: 1 marks a fixed node.
All inputs are finite; a program needn't handle non-finite values. No bound on the sum of `solid_mask` or of `fixed_mask` on one device may be relied on, other than what follows from the above.
Results may differ from a plain program's by a relative error of at most 0.0001.
Values sent between devices are 32-bit elements; how exact they have to be, the bound alone decides.
A program may use at most 64 MiB of HBM per device.

v0:
```python
import jax
import jax.numpy as jnp
import numpy as np
from jax import lax
from jax.sharding import PartitionSpec as P

void_stiffness = 0.001


def from_behind(value, axis, steps):
    count = lax.axis_size(axis)
    first, last = (max(0, -steps), min(count, count - steps))
    return lax.ppermute(value, axis, [(source, source + steps) for source in range(first, last)])


def element_matrix():
    poisson = 0.3
    lame_first = poisson / ((1.0 + poisson) * (1.0 - 2.0 * poisson))
    shear_mod = 1.0 / (2.0 * (1.0 + poisson))
    elastic = np.zeros((6, 6))
    elastic[:3, :3] = lame_first
    for k in range(3):
        elastic[k, k] = lame_first + 2.0 * shear_mod
    for k in range(3, 6):
        elastic[k, k] = shear_mod
    points = [(1.0 - 1.0 / np.sqrt(3.0)) / 2.0, (1.0 + 1.0 / np.sqrt(3.0)) / 2.0]
    matrix = np.zeros((24, 24))
    for a in points:
        for b in points:
            for d in points:
                strain = np.zeros((6, 24))
                for c in range(8):
                    ox, oy, oz = (c % 2, c // 2 % 2, c // 4)
                    weight_x = a if ox else 1.0 - a
                    weight_y = b if oy else 1.0 - b
                    weight_z = d if oz else 1.0 - d
                    slope_x = (1.0 if ox else -1.0) * weight_y * weight_z
                    slope_y = (1.0 if oy else -1.0) * weight_x * weight_z
                    slope_z = (1.0 if oz else -1.0) * weight_x * weight_y
                    strain[0, 3 * c] = slope_x
                    strain[1, 3 * c + 1] = slope_y
                    strain[2, 3 * c + 2] = slope_z
                    strain[3, 3 * c] = slope_y
                    strain[3, 3 * c + 1] = slope_x
                    strain[4, 3 * c + 1] = slope_z
                    strain[4, 3 * c + 2] = slope_y
                    strain[5, 3 * c] = slope_z
                    strain[5, 3 * c + 2] = slope_x
                matrix = matrix + strain.T @ elastic @ strain / 8.0
    return matrix.reshape(8, 3, 8, 3)


def shift_ahead(values, along):
    count = values.shape[along]
    rest = lax.slice_in_dim(values, 1, count, axis=along)
    edge = jnp.zeros_like(lax.slice_in_dim(values, 0, 1, axis=along))
    return jnp.concatenate([rest, edge], axis=along)


def shift_behind(values, along):
    count = values.shape[along]
    rest = lax.slice_in_dim(values, 0, count - 1, axis=along)
    edge = jnp.zeros_like(lax.slice_in_dim(values, 0, 1, axis=along))
    return jnp.concatenate([edge, rest], axis=along)


def element_stiffness(densities, solid_mask, start_layer, total_layers):
    full_shape = densities.shape
    depth_index = lax.broadcasted_iota(jnp.int32, full_shape, 0) + start_layer
    across_x = lax.broadcasted_iota(jnp.int32, full_shape, 1)
    across_y = lax.broadcasted_iota(jnp.int32, full_shape, 2)
    inside = (
        (depth_index < total_layers - 1)
        & (across_x < full_shape[1] - 1)
        & (across_y < full_shape[2] - 1)
    )
    values = solid_mask.astype(jnp.float32) * densities**3 + void_stiffness
    return jnp.where(inside, values, 0.0)


def element_forces(extended, stiffness, matrix):
    layers = stiffness.shape[0]
    corner_views = []
    for c in range(8):
        view = lax.slice_in_dim(extended, c // 4, c // 4 + layers, axis=1)
        if c % 2:
            view = shift_ahead(view, 2)
        if c // 2 % 2:
            view = shift_ahead(view, 3)
        corner_views.append(view)
    stacked = jnp.stack(corner_views)
    forces = (
        jnp.einsum("cadb,dbzxy->cazxy", matrix, stacked, precision=lax.Precision.HIGHEST)
        * stiffness
    )
    result = jnp.zeros(extended.shape, jnp.float32)
    for c in range(8):
        piece = forces[c]
        if c % 2:
            piece = shift_behind(piece, 2)
        if c // 2 % 2:
            piece = shift_behind(piece, 3)
        result = result.at[:, c // 4 : c // 4 + layers].add(piece)
    return result


def apply_operator(columns, free_mask, stiffness):
    matrix = jnp.asarray(element_matrix(), dtype=jnp.float32)
    moved = columns * free_mask
    upper = from_behind(moved[:, :, :1], "slab", -1)
    extended = jnp.concatenate([moved, upper], axis=2)

    def per_column(column):
        return element_forces(column, stiffness, matrix)

    forces_out = lax.map(per_column, extended)
    spilled = from_behind(forces_out[:, :, -1:], "slab", 1)
    interior = jnp.concatenate([forces_out[:, :, :1] + spilled, forces_out[:, :, 1:-1]], axis=2)
    return free_mask * interior + (1.0 - free_mask) * columns


def factor_gram(gram_matrix, total_cols):
    cholesky_lower = jnp.linalg.cholesky(gram_matrix)
    inverse = lax.linalg.triangular_solve(
        cholesky_lower, jnp.eye(total_cols, dtype=jnp.float32), left_side=True, lower=True
    )
    return (cholesky_lower, inverse)


def on_device(recycle_basis, densities, solid_mask, fixed_mask):
    layers = recycle_basis.shape[2]
    slab_count = lax.axis_size("slab")
    col_count = lax.axis_size("col")
    own_count = recycle_basis.shape[0]
    total_cols = own_count * col_count
    col_first = lax.axis_index("col") * own_count
    free_mask = 1.0 - fixed_mask.astype(jnp.float32)
    stiffness = element_stiffness(
        densities, solid_mask, lax.axis_index("slab") * layers, layers * slab_count
    )
    gathered = lax.all_gather(recycle_basis, "col", axis=0, tiled=True)
    image_full = apply_operator(gathered, free_mask, stiffness)
    flattened = image_full.reshape(total_cols, -1)
    rows_total = flattened.shape[1] * slab_count
    gram_part = lax.dot_general(
        flattened,
        flattened,
        (((1,), (1,)), ((), ())),
        precision=lax.Precision.HIGHEST,
        preferred_element_type=jnp.float32,
    )
    gram_matrix = lax.psum(gram_part, "slab")
    gram_matrix = gram_matrix / rows_total
    cholesky_lower, inverse = factor_gram(gram_matrix, total_cols)
    own_inverse = lax.dynamic_slice_in_dim(inverse, col_first, own_count, 0)
    ortho = jnp.dot(
        own_inverse, flattened, precision=lax.Precision.HIGHEST, preferred_element_type=jnp.float32
    ).reshape(recycle_basis.shape)
    renewed = jnp.dot(
        own_inverse,
        gathered.reshape(total_cols, -1),
        precision=lax.Precision.HIGHEST,
        preferred_element_type=jnp.float32,
    ).reshape(recycle_basis.shape)
    return (ortho, renewed, cholesky_lower.T)


def solution(mesh):
    placed = (
        P("col", None, "slab", None, None),
        P("slab", None, None),
        P("slab", None, None),
        P("slab", None, None),
    )
    return jax.shard_map(
        on_device,
        mesh=mesh,
        in_specs=placed,
        out_specs=(P("col", None, "slab", None, None), P("col", None, "slab", None, None), P()),
        check_vma=False,
    )
```

profile of v0, /device:TPU:1, one launch (start us, length us, event | category | flops | bytes accessed | tf_op | source)
XLA Modules:
  0.0 229.1 jit_solution(9076592694379909722)
XLA Ops:
  0.6 13.1 %all_gather.3 = f32[16,3,2,8,256]{4,3,2,1,0:T(8,128)S(1)} all-gather(f32[4,3,2,8,256]{4,3,2,1,0:T(8,128)} %param.23), channel_id=1, replica_groups=mesh['slab'=64,'col'=4] {'col'}, dimensions={0}, use_global_device_ids=true | all-gather | bytes 983040 | tf_op jit(solution)/shard_map/all_gather | solution.py:141
  13.7 0.7 broadcast_subtract_fusion
  14.6 6.2 %collective-permute-start = (f32[16,3,1,8,256]{4,3,2,1,0:T(8,128)S(1)}, f32[16,3,1,8,256]{4,3,2,1,0:T(8,128)S(1)}, u32[]{:S(2)}, u32[]{:S(2)}) collective-permute-start(f32[16,3,1,8,256]{4,3,2,1,0:T(8,128)S(1)} %slice.472), channel_id=1, source_target_pairs={{4,0},{8,4},{12,8},{16,12},{20,16},{24,20},{28,24},{32,28},{36,32}... | collective-permute-start | bytes 1179656 | tf_op jit(solution)/shard_map/ppermute | solution.py:13
  20.9 4.5 %collective-permute-done = f32[16,3,1,8,256]{4,3,2,1,0:T(8,128)S(1)} collective-permute-done((f32[16,3,1,8,256]{4,3,2,1,0:T(8,128)S(1)}, f32[16,3,1,8,256]{4,3,2,1,0:T(8,128)S(1)}, u32[]{:S(2)}, u32[]{:S(2)}) %collective-permute-start) | collective-permute-done | bytes 393248 | tf_op jit(solution)/shard_map/ppermute | solution.py:13
  25.5 54.7 %while.21 = (s32[]{:T(128)}, f32[16,3,3,8,256]{4,3,2,1,0:T(8,128)}, f32[16,3,3,8,256]{4,3,2,1,0:T(8,128)S(1)}, f32[2,8,256]{2,1,0:T(8,128)S(1)}, s32[]{:T(128)}, /*index=5*/f32[8,3,8,3,1,1]{2,0,3,1,5,4:T(8,128)S(1)}, f32[]{:T(128)}) while((s32[]{:T(128)}, f32[16,3,3,8,256]{4,3,2,1,0:T(8,128)}, ...), condition=%wide.region_1.2_spmd.clone, body=%wide.region_0.1_spmd.sunk.clone.sunk | while | flops 28569600 | bytes 7303765 | solution.py:116
  26.3 0.6 stack.73
  28.3 0.6 constant_dynamic-update-slice_fusion.5
  38.6 0.6 constant_dynamic-update-slice_fusion.5
  42.0 0.6 constant_dynamic-update-slice_fusion.5
  43.4 0.6 stack.73
  46.8 0.6 stack.73
  50.2 0.6 stack.73
  53.6 0.6 stack.73
  57.1 0.6 stack.73
  63.9 0.6 stack.73
  65.9 0.6 constant_dynamic-update-slice_fusion.5
  79.6 0.6 constant_dynamic-update-slice_fusion.5
  80.2 1.0 slice.399
  81.2 1.9 collective-permute-start.1
  83.2 4.7 %collective-permute-done.1 = f32[16,3,1,8,256]{4,3,2,1,0:T(8,128)S(1)} collective-permute-done((f32[16,3,1,8,256]{4,3,2,1,0:T(8,128)S(1)}, f32[16,3,1,8,256]{4,3,2,1,0:T(8,128)S(1)}, u32[]{:S(2)}, u32[]{:S(2)}) %collective-permute-start.1) | collective-permute-done | bytes 393248 | tf_op jit(solution)/shard_map/ppermute | solution.py:13
  87.9 1.2 slice_add_fusion.1
  89.3 1.4 convolution_bitcast_fusion.1
  90.8 130.1 %psum.7 = f32[16,16]{0,1:T(8,128)S(1)} all-reduce(f32[16,16]{0,1:T(8,128)S(1)} %convolution_bitcast_fusion.1), channel_id=1, replica_groups=mesh['slab'=64,'col'=4] {'slab'}, use_global_device_ids=true, to_apply=%region_2.3 | all-reduce | flops 256 | bytes 2048 | tf_op jit(solution)/shard_map/psum | solution.py:152
  220.9 1.5 cholesky.17
  222.4 0.6 compare_reduce_fusion
  223.1 0.6 fusion.16
  223.7 1.2 custom-call.6
  225.2 0.9 fusion.5
  226.1 0.7 copy.316
  226.8 0.9 fusion.7
  227.7 0.7 copy.315
  228.4 0.7 copy.317
  (633 shorter events, 43.8 us)
Async XLA Ops:
  14.5 6.3 %copy-start.1 = (f32[2,8,256]{2,1,0:T(8,128)S(1)}, f32[2,8,256]{2,1,0:T(8,128)}, u32[]{:S(2)}) copy-start(f32[2,8,256]{2,1,0:T(8,128)} %param.24) | copy-start | bytes 49156
  14.5 6.3 %copy-start.2 = (s32[2,8,256]{2,1,0:T(8,128)S(1)}, s32[2,8,256]{2,1,0:T(8,128)}, u32[]{:S(2)}) copy-start(s32[2,8,256]{2,1,0:T(8,128)} %param.25) | copy-start | bytes 49156
  14.6 10.8 %collective-permute-start = (f32[16,3,1,8,256]{4,3,2,1,0:T(8,128)S(1)}, f32[16,3,1,8,256]{4,3,2,1,0:T(8,128)S(1)}, u32[]{:S(2)}, u32[]{:S(2)}) collective-permute-start(f32[16,3,1,8,256]{4,3,2,1,0:T(8,128)S(1)} %slice.472), channel_id=1, source_target_pairs={{4,0},{8,4},{12,8},{16,12},{20,16},{24,20},{28,24},{32,28},{36,32}... | collective-permute-start | bytes 1179656 | tf_op jit(solution)/shard_map/ppermute | solution.py:13
  20.9 4.6 %copy-start = (f32[8,3,8,3,1,1]{2,0,3,1,5,4:T(8,128)S(1)}, f32[8,3,8,3,1,1]{2,0,3,1,5,4:T(8,128)}, u32[]{:S(2)}) copy-start(f32[8,3,8,3,1,1]{2,0,3,1,5,4:T(8,128)} %constant.380) | copy-start | bytes 6916
  81.2 6.6 %collective-permute-start.1 = (f32[16,3,1,8,256]{4,3,2,1,0:T(8,128)S(1)}, f32[16,3,1,8,256]{4,3,2,1,0:T(8,128)S(1)}, u32[]{:S(2)}, u32[]{:S(2)}) collective-permute-start(f32[16,3,1,8,256]{4,3,2,1,0:T(8,128)S(1)} %slice.399), channel_id=1, source_target_pairs={{0,4},{4,8},{8,12},{12,16},{16,20},{20,24},{24,28},{28,32},{32,36}... | collective-permute-start | bytes 1179656 | tf_op jit(solution)/shard_map/ppermute | solution.py:13
where the time goes:
time: 229 us
  blocking collectives  143 us (62%)
  local copies, waits for them, and re-layouts  39.3 us (17%)
  other arithmetic  12.7 us (6%)
  matrix products  11.7 us (5%)
  waiting for transfers between devices  9.18 us (4%)
  starting transfers between devices  8.08 us (4%)
  loops' own time  4.12 us (2%)
    psum x1, blocking collectives, on_device(): gram_matrix = lax.psum(gram_part, 'slab')  130 us
    another operation x224, local copies, waits for them, and re-layouts, element_forces(): stacked = jnp.stack(corner_views)  17.6 us
    all_gather x1, blocking collectives, on_device(): gathered = lax.all_gather(recycle_basis, 'col', axis=0, tiled=True)  13.1 us
    dynamic_update_slice x16, local copies, waits for them, and re-layouts, apply_operator(): forces_out = lax.map(per_column, extended)  10.2 us
    ppermute x2, waiting for transfers between devices, from_behind(): lax.ppermute(value, axis, [(source, source + steps) for source in range(f...  9.18 us
    dot_general x16, matrix products, element_forces(): jnp.einsum('cadb,dbzxy->cazxy', matrix, stacked, precision=lax.Precision....  8.3 us
    ppermute x2, starting transfers between devices, from_behind(): lax.ppermute(value, axis, [(source, source + steps) for source in range(f...  8.08 us
    scatter-add x112, other arithmetic, element_forces(): result = result.at[:, c // 4:c // 4 + layers].add(piece)  6.21 us
  transfers between devices with their start and end apart: 2, of which 2 were waited for; matrix products, arithmetic and copies ran while one was open for 0% of the time, Pallas kernels for 0%

commit v1 on v0

--- a/solution.py
+++ b/solution.py
@@ -149,7 +149,7 @@
         precision=lax.Precision.HIGHEST,
         preferred_element_type=jnp.float32,
     )
-    gram_matrix = lax.psum(gram_part, "slab")
+    gram_matrix = jnp.sum(lax.all_gather(gram_part, "slab"), axis=0)
     gram_matrix = gram_matrix / rows_total
     cholesky_lower, inverse = factor_gram(gram_matrix, total_cols)
     own_inverse = lax.dynamic_slice_in_dim(inverse, col_first, own_count, 0)

time: 229 us -> 157 us (0.69)
  blocking collectives: 143 us -> 70.6 us
    psum x1 -> x0, blocking collectives: 130 us -> none  [on_device(): gram_matrix = lax.psum(gram_part, 'slab')]
    all_gather x0 -> x1, blocking collectives: none -> 57.5 us  [on_device(): gram_matrix = jnp.sum(lax.all_gather(gram_part, 'slab'), axis=0)]
where the time goes in v1:
time: 157 us
  blocking collectives  70.6 us (45%)
  local copies, waits for them, and re-layouts  39.4 us (25%)
  other arithmetic  12.8 us (8%)
  matrix products  11.7 us (7%)
  waiting for transfers between devices  9.18 us (6%)
  starting transfers between devices  8.08 us (5%)
  loops' own time  4.12 us (3%)
    all_gather x1, blocking collectives, on_device(): gram_matrix = jnp.sum(lax.all_gather(gram_part, 'slab'), axis=0)  57.5 us
    another operation x224, local copies, waits for them, and re-layouts, element_forces(): stacked = jnp.stack(corner_views)  17.6 us
    all_gather x1, blocking collectives, on_device(): gathered = lax.all_gather(recycle_basis, 'col', axis=0, tiled=True)  13.1 us
    dynamic_update_slice x16, local copies, waits for them, and re-layouts, apply_operator(): forces_out = lax.map(per_column, extended)  10.2 us
    ppermute x2, waiting for transfers between devices, from_behind(): lax.ppermute(value, axis, [(source, source + steps) for source in range(f...  9.18 us
    dot_general x16, matrix products, element_forces(): jnp.einsum('cadb,dbzxy->cazxy', matrix, stacked, precision=lax.Precision....  8.3 us
    ppermute x2, starting transfers between devices, from_behind(): lax.ppermute(value, axis, [(source, source + steps) for source in range(f...  8.08 us
    scatter-add x112, other arithmetic, element_forces(): result = result.at[:, c // 4:c // 4 + layers].add(piece)  6.21 us
  transfers between devices with their start and end apart: 2, of which 2 were waited for; matrix products, arithmetic and copies ran while one was open for 0% of the time, Pallas kernels for 0%

profile of v1, /device:TPU:1, one launch (start us, length us, event | category | flops | bytes accessed | tf_op | source)
XLA Modules:
  0.0 156.6 jit_solution(3483695893704885601)
XLA Ops:
  0.6 13.1 %all_gather.9 = f32[16,3,2,8,256]{4,3,2,1,0:T(8,128)S(1)} all-gather(f32[4,3,2,8,256]{4,3,2,1,0:T(8,128)} %param.23), channel_id=1, replica_groups=mesh['slab'=64,'col'=4] {'col'}, dimensions={0}, use_global_device_ids=true | all-gather | bytes 983040 | tf_op jit(solution)/shard_map/all_gather | solution.py:141
  13.7 0.7 broadcast_subtract_fusion
  14.6 6.2 %collective-permute-start = (f32[16,3,1,8,256]{4,3,2,1,0:T(8,128)S(1)}, f32[16,3,1,8,256]{4,3,2,1,0:T(8,128)S(1)}, u32[]{:S(2)}, u32[]{:S(2)}) collective-permute-start(f32[16,3,1,8,256]{4,3,2,1,0:T(8,128)S(1)} %slice.472), channel_id=1, source_target_pairs={{4,0},{8,4},{12,8},{16,12},{20,16},{24,20},{28,24},{32,28},{36,32}... | collective-permute-start | bytes 1179656 | tf_op jit(solution)/shard_map/ppermute | solution.py:13
  20.9 4.5 %collective-permute-done = f32[16,3,1,8,256]{4,3,2,1,0:T(8,128)S(1)} collective-permute-done((f32[16,3,1,8,256]{4,3,2,1,0:T(8,128)S(1)}, f32[16,3,1,8,256]{4,3,2,1,0:T(8,128)S(1)}, u32[]{:S(2)}, u32[]{:S(2)}) %collective-permute-start) | collective-permute-done | bytes 393248 | tf_op jit(solution)/shard_map/ppermute | solution.py:13
  25.5 54.7 %while.21 = (s32[]{:T(128)}, f32[16,3,3,8,256]{4,3,2,1,0:T(8,128)}, f32[16,3,3,8,256]{4,3,2,1,0:T(8,128)S(1)}, f32[2,8,256]{2,1,0:T(8,128)S(1)}, s32[]{:T(128)}, /*index=5*/f32[8,3,8,3,1,1]{2,0,3,1,5,4:T(8,128)S(1)}, f32[]{:T(128)}) while((s32[]{:T(128)}, f32[16,3,3,8,256]{4,3,2,1,0:T(8,128)}, ...), condition=%wide.region_1.2_spmd.clone, body=%wide.region_0.1_spmd.sunk.clone.sunk | while | flops 28569600 | bytes 7303765 | solution.py:116
  26.3 0.6 stack.73
  28.3 0.6 constant_dynamic-update-slice_fusion.5
  38.6 0.6 constant_dynamic-update-slice_fusion.5
  42.0 0.6 constant_dynamic-update-slice_fusion.5
  43.4 0.6 stack.73
  46.8 0.6 stack.73
  50.2 0.6 stack.73
  53.6 0.6 stack.73
  57.1 0.6 stack.73
  63.9 0.6 stack.73
  65.9 0.6 constant_dynamic-update-slice_fusion.5
  79.6 0.6 constant_dynamic-update-slice_fusion.5
  80.2 1.0 slice.399
  81.2 1.9 %collective-permute-start.1 = (f32[16,3,1,8,256]{4,3,2,1,0:T(8,128)S(1)}, f32[16,3,1,8,256]{4,3,2,1,0:T(8,128)S(1)}, u32[]{:S(2)}, u32[]{:S(2)}) collective-permute-start(f32[16,3,1,8,256]{4,3,2,1,0:T(8,128)S(1)} %slice.399), channel_id=1, source_target_pairs={{0,4},{4,8},{8,12},{12,16},{16,20},{20,24},{24,28},{28,32},{32,36}... | collective-permute-start | bytes 1179656 | tf_op jit(solution)/shard_map/ppermute | solution.py:13
  83.2 4.7 %collective-permute-done.1 = f32[16,3,1,8,256]{4,3,2,1,0:T(8,128)S(1)} collective-permute-done((f32[16,3,1,8,256]{4,3,2,1,0:T(8,128)S(1)}, f32[16,3,1,8,256]{4,3,2,1,0:T(8,128)S(1)}, u32[]{:S(2)}, u32[]{:S(2)}) %collective-permute-start.1) | collective-permute-done | bytes 393248 | tf_op jit(solution)/shard_map/ppermute | solution.py:13
  87.9 1.2 slice_add_fusion.1
  89.3 1.4 convolution_bitcast_fusion.1
  90.7 57.5 %all-gather = f32[1024,16]{1,0:T(8,128)S(1)} all-gather(f32[16,16]{1,0:T(8,128)S(1)} %convolution_bitcast_fusion.1), channel_id=2, replica_groups=mesh['slab'=64,'col'=4] {'slab'}, dimensions={0}, use_global_device_ids=true | all-gather | bytes 66560 | tf_op jit(solution)/shard_map/all_gather | solution.py:152
  148.5 1.5 cholesky.17
  150.0 0.6 compare_reduce_fusion
  150.6 0.6 fusion.16
  151.3 1.2 custom-call.6
  152.7 0.9 fusion.5
  153.6 0.7 copy.307
  154.3 0.9 fusion.7
  155.3 0.7 copy.306
  156.0 0.7 copy.308
  (635 shorter events, 43.9 us)
Async XLA Ops:
  14.5 6.3 %copy-start.1 = (f32[2,8,256]{2,1,0:T(8,128)S(1)}, f32[2,8,256]{2,1,0:T(8,128)}, u32[]{:S(2)}) copy-start(f32[2,8,256]{2,1,0:T(8,128)} %param.24) | copy-start | bytes 49156
  14.5 6.3 %copy-start.2 = (s32[2,8,256]{2,1,0:T(8,128)S(1)}, s32[2,8,256]{2,1,0:T(8,128)}, u32[]{:S(2)}) copy-start(s32[2,8,256]{2,1,0:T(8,128)} %param.25) | copy-start | bytes 49156
  14.6 10.8 %collective-permute-start = (f32[16,3,1,8,256]{4,3,2,1,0:T(8,128)S(1)}, f32[16,3,1,8,256]{4,3,2,1,0:T(8,128)S(1)}, u32[]{:S(2)}, u32[]{:S(2)}) collective-permute-start(f32[16,3,1,8,256]{4,3,2,1,0:T(8,128)S(1)} %slice.472), channel_id=1, source_target_pairs={{4,0},{8,4},{12,8},{16,12},{20,16},{24,20},{28,24},{32,28},{36,32}... | collective-permute-start | bytes 1179656 | tf_op jit(solution)/shard_map/ppermute | solution.py:13
  20.9 4.6 %copy-start = (f32[8,3,8,3,1,1]{2,0,3,1,5,4:T(8,128)S(1)}, f32[8,3,8,3,1,1]{2,0,3,1,5,4:T(8,128)}, u32[]{:S(2)}) copy-start(f32[8,3,8,3,1,1]{2,0,3,1,5,4:T(8,128)} %constant.380) | copy-start | bytes 6916
  81.2 6.6 %collective-permute-start.1 = (f32[16,3,1,8,256]{4,3,2,1,0:T(8,128)S(1)}, f32[16,3,1,8,256]{4,3,2,1,0:T(8,128)S(1)}, u32[]{:S(2)}, u32[]{:S(2)}) collective-permute-start(f32[16,3,1,8,256]{4,3,2,1,0:T(8,128)S(1)} %slice.399), channel_id=1, source_target_pairs={{0,4},{4,8},{8,12},{12,16},{16,20},{20,24},{24,28},{28,32},{32,36}... | collective-permute-start | bytes 1179656 | tf_op jit(solution)/shard_map/ppermute | solution.py:13
